TPU v7x, 128 devices: a whole 4x4x4 slice. The times are simulated.
128 devices in a mesh: seq: 16 (over z, x), head: 8 (over y, core).
Axes of the slice: x: 4, y: 4, z: 4, core: 2. Of those that a mesh axis runs over, the one named last changes fastest.
Arguments:
- tokens: bfloat16 [16384, 4096], P('seq'), may hold values from -6 to 6
- w_query: bfloat16 [4096, 4096], P(None, 'head'), may hold values from -0.09375 to 0.09375
- w_key: bfloat16 [4096, 4096], P(None, 'head'), may hold values from -0.09375 to 0.09375
- w_value: bfloat16 [4096, 4096], P(None, 'head'), may hold values from -0.09375 to 0.09375
- norm_gain: float32 [4096], P('head'), may hold values from 0.25 to 1.75
- w_out: bfloat16 [4096, 4096], P('head'), may hold values from -0.125 to 0.125
Outputs:
- mixed: bfloat16 [16384, 4096], P('seq', 'head')
All inputs are finite; a program needn't handle non-finite values.
Results may differ from a plain program's by a relative error of at most 0.02.
Values may be sent and summed in bfloat16 or wider, within the bound.
No kernel may reach another device: no remote copies, remote signals or barrier semaphores. Data moves between devices by JAX's collectives and lax.ppermute only.
A program may use at most 128 MiB of HBM per device.

v0:
```python
import jax
import jax.numpy as jnp
from jax import lax
from jax.experimental import pallas as pl
from jax.experimental.pallas import tpu as pltpu
from jax.sharding import PartitionSpec as P


HEAD_DIM = 128
BLOCK = 256
RING = 4
SETS = 2
F32, BF16 = jnp.float32, jnp.bfloat16
IN_VMEM = pl.BlockSpec(memory_space=pltpu.VMEM)
IN_HBM = pl.BlockSpec(memory_space=pltpu.HBM)
IN_SMEM = pl.BlockSpec(memory_space=pltpu.SMEM)


def dot(a, b):
    return jnp.dot(a, b, preferred_element_type=F32)


def dot_t(a, b, da, db):
    return lax.dot_general(a, b, (((da,), (db,)), ((), ())), preferred_element_type=F32)


def call(kernel, in_specs, out_shape, args, flops, nbytes, mib, scratch=(), aliases=None):
    return pl.pallas_call(
        kernel,
        in_specs=in_specs,
        out_specs=jax.tree.map(lambda _: IN_VMEM, out_shape),
        out_shape=out_shape,
        scratch_shapes=scratch,
        compiler_params=pltpu.CompilerParams(vmem_limit_bytes=mib * 2**20),
        cost_estimate=pl.CostEstimate(
            flops=int(flops), bytes_accessed=int(nbytes), transcendentals=0
        ),
        input_output_aliases=aliases or {},
    )(*args)


def held(x):
    return pltpu.with_memory_space_constraint(x, pltpu.VMEM)


def streamed(x):
    return pltpu.with_memory_space_constraint(x, pltpu.HBM)


SLOTS = 3


def project(tokens, weights, ranges, states=False, after=()):
    depth = tokens.shape[1]
    width = weights[0].shape[1]
    count = sum(size for _, size in ranges)
    places = [sum(size for _, size in ranges[:r]) for r in range(len(ranges))]
    n_w, n_r = len(weights), len(ranges)
    big = depth // 4
    sizes = [big // 2, big // 2] + [big] * 3
    starts = [sum(sizes[:k]) for k in range(len(sizes))]
    steps = len(sizes)

    def kernel(*refs):
        t_hbm, w_hbm = refs[0], refs[1 : 1 + n_w]
        rest = refs[1 + n_w + len(after) :]
        outs, rest = rest[:n_w], rest[n_w:]
        if states:
            s_ref, rest = rest[0], rest[1:]
        t_buf, w_buf, acc, t_sem, w_sem = rest

        def copies(k):
            at, size, slot = pl.ds(starts[k], sizes[k]), pl.ds(0, sizes[k]), k % SLOTS
            moves = []
            for r, (first, tall) in enumerate(ranges):
                moves.append(
                    pltpu.make_async_copy(
                        t_hbm.at[pl.ds(first, tall), at],
                        t_buf.at[slot, pl.ds(places[r], tall), size],
                        t_sem.at[k, r],
                    )
                )
            for i in range(n_w):
                moves.append(
                    pltpu.make_async_copy(
                        w_hbm[i].at[at, :], w_buf.at[slot, i, size, :], w_sem.at[k, i]
                    )
                )
            return moves

        for k in range(SLOTS - 1):
            for move in copies(k):
                move.start()
        for k in range(steps):
            for move in copies(k):
                move.wait()
            if k + SLOTS - 1 < steps:
                for move in copies(k + SLOTS - 1):
                    move.start()
            slot, size = k % SLOTS, sizes[k]
            for i in range(n_w):
                product = dot(t_buf[slot, :, :size], w_buf[slot, i, :size, :])
                if k == 0:
                    acc[i] = product
                elif k < steps - 1:
                    acc[i] += product
                else:
                    outs[i][...] = (acc[i] + product).astype(BF16)
        if states:
            for h in range(width // HEAD_DIM):
                cols = slice(h * HEAD_DIM, (h + 1) * HEAD_DIM)
                s_ref[cols, :] = dot_t(outs[0][:, cols], outs[1][:, cols], 0, 0).astype(BF16)

    out_shape = [pltpu.VMEM((count, width), BF16)] * n_w
    if states:
        out_shape = out_shape + [pltpu.VMEM((width, HEAD_DIM), BF16)]
    return call(
        kernel,
        [IN_HBM] * (1 + n_w) + [pl.BlockSpec(memory_space=pl.ANY)] * len(after),
        out_shape,
        (streamed(tokens), *map(streamed, weights), *after),
        2 * count * depth * width * n_w,
        2 * depth * (count + width * n_w),
        28,
        [
            pltpu.VMEM((SLOTS, count, big), BF16),
            pltpu.VMEM((SLOTS, n_w, big, width), BF16),
            pltpu.VMEM((n_w, count, width), F32),
            pltpu.SemaphoreType.DMA((steps, n_r)),
            pltpu.SemaphoreType.DMA((steps, n_w)),
        ],
    )


def row_total(total, came, after):
    def kernel(*refs):
        refs[-1][...] = sum((r[...].astype(F32) for r in refs[1:-2]), refs[0][...].astype(F32)).astype(
            BF16
        )

    return call(
        kernel,
        [IN_VMEM] * (1 + len(came)) + [pl.BlockSpec(memory_space=pl.ANY)],
        pltpu.VMEM(total.shape, BF16),
        (total, *came, after),
        4 * total.size,
        8 * total.size,
        4,
    )


def local_attention(part, q, k, v, bring=(), after=()):
    rows_q, width = q.shape
    heads = width // HEAD_DIM
    blocks = k.shape[0] // BLOCK
    mine = set_blocks(part, blocks)
    n_b = len(bring)

    def kernel(q_ref, k_ref, v_ref, *refs):
        b_hbm, rest = refs[:n_b], refs[n_b + len(after) :]
        w_ref = rest[0]
        moves = []
        if bring:
            e_ref, b_ref, sem = rest[1:]
            deep = b_hbm[0].shape[0]
            moves = [
                pltpu.make_async_copy(source, b_ref.at[pl.ds(i * deep, deep), :], sem.at[i])
                for i, source in enumerate(b_hbm)
            ]
        for move in moves:
            move.start()
        rows = lax.broadcasted_iota(jnp.int32, (BLOCK, BLOCK), 0)
        cols = lax.broadcasted_iota(jnp.int32, (BLOCK, BLOCK), 1)
        keep = rows >= cols
        for h in range(heads):
            at_h = slice(h * HEAD_DIM, (h + 1) * HEAD_DIM)
            state = jnp.zeros((HEAD_DIM, HEAD_DIM), F32)
            for b in range(blocks):
                at = slice(b * BLOCK, (b + 1) * BLOCK)
                kb, vb = k_ref[at, at_h], v_ref[at, at_h]
                if b in mine:
                    at_q = slice(mine.index(b) * BLOCK, (mine.index(b) + 1) * BLOCK)
                    scores = jnp.where(keep, dot_t(q_ref[at_q, at_h], kb, 1, 1), 0.0)
                    w_ref[at_q, at_h] = dot(scores.astype(BF16), vb)
                if bring:
                    e_ref[b, at_h, :] = state
                    if b < blocks - 1:
                        state = state + dot_t(kb, vb, 0, 0)
        for move in moves:
            move.wait()

    out_shape = [pltpu.VMEM((rows_q, width), F32)]
    scratch, nbytes = [], 14 * rows_q * width
    if bring:
        deep, wide = bring[0].shape
        out_shape.append(pltpu.VMEM((blocks, width, HEAD_DIM), F32))
        out_shape.append(pltpu.VMEM((n_b * deep, wide), BF16))
        scratch = [pltpu.SemaphoreType.DMA((n_b,))]
        nbytes += 2 * n_b * deep * wide
    return call(
        kernel,
        [IN_VMEM] * 3
        + [IN_HBM] * n_b
        + [pl.BlockSpec(memory_space=pl.ANY)] * len(after),
        out_shape,
        (q, k, v, *map(streamed, bring), *after),
        4 * rows_q * width * (BLOCK + HEAD_DIM),
        nbytes,
        12,
        scratch,
    )


def set_blocks(part, blocks):
    per_half = blocks // 2 // SETS
    return [half * (blocks // 2) + part * per_half + b for half in range(2) for b in range(per_half)]


def attend(part, place, index, q, within, earlier, from_x, from_z, gain, mine):
    count, width = q.shape
    heads = width // HEAD_DIM
    per_half = count // BLOCK // 2
    hops = len(SHIFTS)

    def kernel(place_ref, index_ref, q_ref, w_ref, e_ref, *refs):
        xs, zs, g_ref, o_ref = refs[:hops], refs[hops : 2 * hops], refs[2 * hops], refs[-1]
        half = place_ref[0] % 2 if mine else 1 - place_ref[0] % 2
        at_x, at_z = index_ref[0] % RING, index_ref[0] // RING
        for h in range(heads):
            cols = slice(h * HEAD_DIM, (h + 1) * HEAD_DIM)
            carried = jnp.zeros((HEAD_DIM, HEAD_DIM), F32)
            for at, came in ((at_x, xs), (at_z, zs)):
                for shift, ref in zip(SHIFTS, came):
                    source = (at - shift + RING) % RING
                    carried += jnp.where(source < at, ref[cols, :].astype(F32), 0.0)
            for b in range(per_half):
                here = half * per_half + b
                rows = pl.ds(pl.multiple_of(here * BLOCK, BLOCK), BLOCK)
                block = (half * SETS + part) * per_half + b
                prior = (carried + e_ref[block, cols, :]).astype(BF16)
                raw = w_ref[rows, cols] + dot(q_ref[rows, cols], prior)
                power = jnp.mean(raw * raw, axis=-1, keepdims=True)
                o_ref[b * BLOCK : (b + 1) * BLOCK, cols] = (
                    raw * lax.rsqrt(power + 1e-06) * g_ref[:, cols]
                ).astype(BF16)

    return call(
        kernel,
        [IN_SMEM] * 2 + [IN_VMEM] * (4 + 2 * hops),
        pltpu.VMEM((count // 2, width), BF16),
        (place, index, q, within, earlier, *from_x, *from_z, gain),
        count * width * HEAD_DIM,
        4 * count * width,
        8,
    )


STRAIGHT, CROSS = 0, 1


def out_project(place, mine, theirs, w_out, blocks, added=(), partial=False):
    terms = [x for x in (mine, theirs) if x is not None]
    rows, width = terms[0].shape

    def kernel(place_ref, *refs):
        xs, w_ref, refs = refs[: len(terms)], refs[len(terms)], refs[len(terms) + 1 :]
        adds, outs = refs[: len(added)], refs[len(added) :]
        y, c = place_ref[0] // 2, place_ref[0] % 2
        for p, (step, side) in enumerate(blocks):
            owner = ((y + step + RING) % RING) * 2 + (c if side == STRAIGHT else 1 - c)
            cols = pl.ds(pl.multiple_of(owner * width, width), width)
            total = adds[p][...].astype(F32) if added else 0.0
            if mine is not None:
                total = total + dot(xs[0][...], w_ref[:width, cols])
            if theirs is not None:
                total = total + dot(xs[-1][...], w_ref[width:, cols])
            outs[p][...] = total.astype(outs[p].dtype)

    return call(
        kernel,
        [IN_SMEM] + [IN_VMEM] * (1 + len(terms) + len(added)),
        [pltpu.VMEM((rows, width), F32 if partial else BF16)] * len(blocks),
        (place, *terms, w_out, *added),
        2 * len(terms) * len(blocks) * rows * width * width,
        2 * len(terms) * len(blocks) * width * width,
        12,
    )


def final_sum(place, part, other, terms, count, into=None):
    rows, width = terms[0].shape

    def kernel(place_ref, *refs):
        total = sum(r[...].astype(F32) for r in refs[1 : len(terms)])
        refs[-1][...] = (refs[0][...].astype(F32) + total).astype(BF16)

    def owner(i, place_ref):
        c = place_ref[0] % 2
        return ((1 - c if other else c) * SETS + part, 0)

    specs = [IN_VMEM] * len(terms)
    args, aliases = (place, *terms), {}
    if into is not None:
        aliases = {len(args): 0}
        specs, args = specs + [pl.BlockSpec(memory_space=pl.ANY)], (*args, into)
    return pl.pallas_call(
        kernel,
        grid_spec=pltpu.PrefetchScalarGridSpec(
            num_scalar_prefetch=1,
            grid=(1,),
            in_specs=specs,
            out_specs=pl.BlockSpec((rows, width), owner),
        ),
        out_shape=jax.ShapeDtypeStruct((count, width), BF16),
        input_output_aliases=aliases,
        compiler_params=pltpu.CompilerParams(vmem_limit_bytes=8 * 2**20),
        cost_estimate=pl.CostEstimate(
            flops=3 * rows * width, bytes_accessed=8 * rows * width, transcendentals=0
        ),
    )(*args)


SHIFTS = (1, -1, 2)


def head_send(x, step, cross=0):
    pairs = [
        (h, ((h // 2 + step) % RING) * 2 + ((h % 2) ^ cross)) for h in range(2 * RING)
    ]
    return held(lax.ppermute(x, "head", pairs))


def seq_send(x, dz, dx):
    pairs = [
        (s, ((s // RING + dz) % RING) * RING + (s % RING + dx) % RING) for s in range(RING * RING)
    ]
    return held(lax.ppermute(x, "seq", pairs))


def local(tokens, w_query, w_key, w_value, norm_gain, w_out):
    count = tokens.shape[0]
    place = lax.axis_index("head").astype(jnp.int32).reshape(1)
    index = lax.axis_index("seq").astype(jnp.int32).reshape(1)

    w_theirs = lax.ppermute(w_out, "head", [(h, h ^ 1) for h in range(2 * RING)])
    keys, values, total = project(
        tokens, [w_key, w_value], [(0, count)], states=True, after=(place, index)
    )
    from_x = [seq_send(total, 0, d) for d in SHIFTS]
    half, rows = count // 2, count // 2 // SETS

    def query(part, after):
        ranges = [(h * half + part * rows, rows) for h in range(2)]
        return project(tokens, [w_query], ranges, after=after)[0]

    queries = query(0, (total,))
    row = row_total(total, from_x, queries)
    from_z = [seq_send(row, d, 0) for d in SHIFTS]
    within, earlier, w_held = local_attention(0, queries, keys, values, (w_out, w_theirs), (row,))
    gain = norm_gain.reshape(1, -1)
    out = None
    for part in range(SETS):
        if part:
            queries = query(part, (within,))
            (within,) = local_attention(part, queries, keys, values)

        def attended(mine):
            return attend(part, place, index, queries, within, earlier, from_x, from_z, gain, mine)

        def send(x, step):
            return head_send(x, step)

        def swap(x):
            return head_send(x, 0, 1)

        theirs = swap(attended(False))
        mine = attended(True)

        def project_out(blocks, mine=mine, theirs=theirs, **kw):
            return out_project(place, mine, theirs, w_held, blocks, **kw)

        blocks = [(2, STRAIGHT), (2, CROSS)]
        begun = project_out(blocks, theirs=None, partial=True)
        far_s, far_x = project_out(blocks, mine=None, added=begun)
        far_s, far_x = send(far_s, -1), send(far_x, 1)
        near_s, near_x = project_out([(1, STRAIGHT), (-1, CROSS)])
        near_s, near_x = send(near_s, 1), send(swap(near_x), -1)
        own_s, own_x = project_out([(0, STRAIGHT), (0, CROSS)])
        own_x = swap(own_x)
        late_s, late_x = project_out([(-1, STRAIGHT), (1, CROSS)], added=(far_s, far_x))
        late_s, late_x = send(late_s, -1), send(swap(late_x), 1)
        out = final_sum(place, part, False, (own_s, near_s, late_s), count, into=out)
        out = final_sum(place, part, True, (own_x, near_x, late_x), count, into=out)
    return out


def solution(mesh):
    in_specs = (
        P("seq", None),
        P(None, "head"),
        P(None, "head"),
        P(None, "head"),
        P("head"),
        P("head", None),
    )
    out_specs = P("seq", "head")
    return jax.shard_map(local, mesh=mesh, in_specs=in_specs, out_specs=out_specs, check_vma=False)
```

profile of v0, /device:TPU:1, one launch (start us, length us, event | category | flops | bytes accessed | tf_op | source)
XLA Modules:
  0.0 94.2 jit_solution(1891700536131823028)
XLA Ops:
  1.4 11.9 %shard_map.64 = (bf16[1024,512]{1,0:T(8,128)(2,1)S(1)}, bf16[1024,512]{1,0:T(8,128)(2,1)S(1)}, bf16[512,128]{1,0:T(8,128)(2,1)S(1)}) custom-call(bf16[1024,4096]{1,0:T(8,128)(2,1)} %refs_0_.7, bf16[4096,512]{1,0:T(8,128)(2,1)} %refs_1_.3, bf16[4096,512]{1,0:T(8,128)(2,1)} %refs_2_.1, s32[1]{0:T(128)} %bitcast.refs_3_.place_ref, s32[1]{0:T(128)} %bitcast.1.refs_4_.index_ref), custom_call_target="tpu_custom_call" | custom-call | flops 8589934592 | bytes 16777216 | tf_op jit(solution)/shard_map/pallas_call | solution.py:28
  13.3 1.4 %collective-permute-start.1 = (bf16[512,128]{1,0:T(8,128)(2,1)S(1)}, bf16[512,128]{1,0:T(8,128)(2,1)S(1)}, u32[]{:S(2)}, u32[]{:S(2)}) collective-permute-start(bf16[512,128]{1,0:T(8,128)(2,1)S(1)} %get-tuple-element.31.refs_2_.refs_0_), channel_id=1, source_target_pairs={{0,8},{8,16},{16,24},{24,0},{32,40},{40,48},{48,56},{56,32},{64,72... | collective-permute-start | bytes 393224 | tf_op jit(solution)/shard_map/ppermute | solution.py:337
  16.1 1.6 %collective-permute-start.3 = (bf16[512,128]{1,0:T(8,128)(2,1)S(1)}, bf16[512,128]{1,0:T(8,128)(2,1)S(1)}, u32[]{:S(2)}, u32[]{:S(2)}) collective-permute-start(bf16[512,128]{1,0:T(8,128)(2,1)S(1)} %get-tuple-element.31.refs_2_.refs_0_), channel_id=1, source_target_pairs={{0,16},{8,24},{16,0},{24,8},{32,48},{40,56},{48,32},{56,40},{64,80... | collective-permute-start | bytes 393224 | tf_op jit(solution)/shard_map/ppermute | solution.py:337
  17.7 5.3 %shard_map.65.refs_4_.q_ref = bf16[512,512]{1,0:T(8,128)(2,1)S(1)} custom-call(bf16[1024,4096]{1,0:T(8,128)(2,1)} %refs_0_.7, bf16[4096,512]{1,0:T(8,128)(2,1)} %refs_1_.5, bf16[512,128]{1,0:T(8,128)(2,1)S(1)} %get-tuple-element.31.refs_2_.refs_0_), custom_call_target="tpu_custom_call" | custom-call | flops 2147483648 | bytes 8388608 | tf_op jit(solution)/shard_map/pallas_call | solution.py:28
  23.6 1.7 %collective-permute-start.4 = (bf16[512,128]{1,0:T(8,128)(2,1)S(1)}, bf16[512,128]{1,0:T(8,128)(2,1)S(1)}, u32[]{:S(2)}, u32[]{:S(2)}) collective-permute-start(bf16[512,128]{1,0:T(8,128)(2,1)S(1)} %shard_map.66.refs_2_), channel_id=1, source_target_pairs={{0,32},{8,40},{16,48},{24,56},{32,64},{40,72},{48,80},{56,88},{64,... | collective-permute-start | bytes 393224 | tf_op jit(solution)/shard_map/ppermute | solution.py:337
  25.4 2.2 %collective-permute-start.5 = (bf16[512,128]{1,0:T(8,128)(2,1)S(1)}, bf16[512,128]{1,0:T(8,128)(2,1)S(1)}, u32[]{:S(2)}, u32[]{:S(2)}) collective-permute-start(bf16[512,128]{1,0:T(8,128)(2,1)S(1)} %shard_map.66.refs_2_), channel_id=1, source_target_pairs={{0,96},{8,104},{16,112},{24,120},{32,0},{40,8},{48,16},{56,24},{64... | collective-permute-start | bytes 393224 | tf_op jit(solution)/shard_map/ppermute | solution.py:337
  28.8 3.5 %shard_map.67 = (f32[512,512]{1,0:T(8,128)S(1)}, f32[4,512,128]{2,1,0:T(8,128)S(1)}, bf16[1024,4096]{1,0:T(8,128)(2,1)S(1)}) custom-call(bf16[512,512]{1,0:T(8,128)(2,1)S(1)} %shard_map.65.refs_4_.q_ref, bf16[1024,512]{1,0:T(8,128)(2,1)S(1)} %get-tuple-element.32.k_ref, bf16[1024,512]{1,0:T(8,128)(2,1)S(1)} %get-tuple-element.33.v_ref, ...), custom_call_target="tpu_custom_call" | custom-call | flops 402653184 | bytes 12058624 | tf_op jit(solution)/shard_map/pallas_call | solution.py:28
  32.3 2.3 %collective-permute-done.6.refs_5_ = bf16[512,128]{1,0:T(8,128)(2,1)S(1)} collective-permute-done((bf16[512,128]{1,0:T(8,128)(2,1)S(1)}, bf16[512,128]{1,0:T(8,128)(2,1)S(1)}, u32[]{:S(2)}, u32[]{:S(2)}) %collective-permute-start.6) | collective-permute-done | bytes 131104 | tf_op jit(solution)/shard_map/ppermute | solution.py:337
  35.1 1.6 %collective-permute-start.17 = (bf16[256,512]{1,0:T(8,128)(2,1)S(1)}, bf16[256,512]{1,0:T(8,128)(2,1)S(1)}, u32[]{:S(2)}, u32[]{:S(2)}) collective-permute-start(bf16[256,512]{1,0:T(8,128)(2,1)S(1)} %shard_map.78), channel_id=1, source_target_pairs={{0,1},{1,0},{2,3},{3,2},{4,5},{5,4},{6,7},{7,6},{8,9},{9,8},{10,11... | collective-permute-start | bytes 786440 | tf_op jit(solution)/shard_map/ppermute | solution.py:330
  36.6 5.3 %shard_map.68.q_ref = bf16[512,512]{1,0:T(8,128)(2,1)S(1)} custom-call(bf16[1024,4096]{1,0:T(8,128)(2,1)} %refs_0_.7, bf16[4096,512]{1,0:T(8,128)(2,1)} %refs_1_.5, f32[512,512]{1,0:T(8,128)S(1)} %get-tuple-element.34.refs_2_.w_ref), custom_call_target="tpu_custom_call" | custom-call | flops 2147483648 | bytes 8388608 | tf_op jit(solution)/shard_map/pallas_call | solution.py:28
  44.9 2.8 %collective-permute-start.21 = (bf16[256,512]{1,0:T(8,128)(2,1)S(1)}, bf16[256,512]{1,0:T(8,128)(2,1)S(1)}, u32[]{:S(2)}, u32[]{:S(2)}) collective-permute-start(bf16[256,512]{1,0:T(8,128)(2,1)S(1)} %get-tuple-element.51), channel_id=1, source_target_pairs={{0,6},{1,7},{2,0},{3,1},{4,2},{5,3},{6,4},{7,5},{8,14},{9,15},{10,... | collective-permute-start | bytes 786440 | tf_op jit(solution)/shard_map/ppermute | solution.py:330
  49.9 2.7 %collective-permute-start.11 = (bf16[256,512]{1,0:T(8,128)(2,1)S(1)}, bf16[256,512]{1,0:T(8,128)(2,1)S(1)}, u32[]{:S(2)}, u32[]{:S(2)}) collective-permute-start(bf16[256,512]{1,0:T(8,128)(2,1)S(1)} %get-tuple-element.41), channel_id=1, source_target_pairs={{0,6},{1,7},{2,0},{3,1},{4,2},{5,3},{6,4},{7,5},{8,14},{9,15},{10,... | collective-permute-start | bytes 786440 | tf_op jit(solution)/shard_map/ppermute | solution.py:330
  53.4 1.5 %collective-permute-start.19 = (bf16[256,512]{1,0:T(8,128)(2,1)S(1)}, bf16[256,512]{1,0:T(8,128)(2,1)S(1)}, u32[]{:S(2)}, u32[]{:S(2)}) collective-permute-start(bf16[256,512]{1,0:T(8,128)(2,1)S(1)} %get-tuple-element.48), channel_id=1, source_target_pairs={{0,1},{1,0},{2,3},{3,2},{4,5},{5,4},{6,7},{7,6},{8,9},{9,8},{10,11... | collective-permute-start | bytes 786440 | tf_op jit(solution)/shard_map/ppermute | solution.py:330
  56.0 2.9 %collective-permute-start.18 = (bf16[256,512]{1,0:T(8,128)(2,1)S(1)}, bf16[256,512]{1,0:T(8,128)(2,1)S(1)}, u32[]{:S(2)}, u32[]{:S(2)}) collective-permute-start(bf16[256,512]{1,0:T(8,128)(2,1)S(1)} %get-tuple-element.47), channel_id=1, source_target_pairs={{0,1},{1,0},{2,3},{3,2},{4,5},{5,4},{6,7},{7,6},{8,9},{9,8},{10,11... | collective-permute-start | bytes 786440 | tf_op jit(solution)/shard_map/ppermute | solution.py:330
  59.6 2.0 %collective-permute-done.25.refs_1_ = bf16[256,512]{1,0:T(8,128)(2,1)S(1)} collective-permute-done((bf16[256,512]{1,0:T(8,128)(2,1)S(1)}, bf16[256,512]{1,0:T(8,128)(2,1)S(1)}, u32[]{:S(2)}, u32[]{:S(2)}) %collective-permute-start.25) | collective-permute-done | bytes 262176 | tf_op jit(solution)/shard_map/ppermute | solution.py:330
  61.6 2.9 %collective-permute-start.23 = (bf16[256,512]{1,0:T(8,128)(2,1)S(1)}, bf16[256,512]{1,0:T(8,128)(2,1)S(1)}, u32[]{:S(2)}, u32[]{:S(2)}) collective-permute-start(bf16[256,512]{1,0:T(8,128)(2,1)S(1)} %get-tuple-element.53), channel_id=1, source_target_pairs={{0,1},{1,0},{2,3},{3,2},{4,5},{5,4},{6,7},{7,6},{8,9},{9,8},{10,11... | collective-permute-start | bytes 786440 | tf_op jit(solution)/shard_map/ppermute | solution.py:330
  65.3 1.9 %collective-permute-done.12.refs_4_ = bf16[256,512]{1,0:T(8,128)(2,1)S(1)} collective-permute-done((bf16[256,512]{1,0:T(8,128)(2,1)S(1)}, bf16[256,512]{1,0:T(8,128)(2,1)S(1)}, u32[]{:S(2)}, u32[]{:S(2)}) %collective-permute-start.12) | collective-permute-done | bytes 262176 | tf_op jit(solution)/shard_map/ppermute | solution.py:330
  68.0 1.7 %collective-permute-start.13 = (bf16[256,512]{1,0:T(8,128)(2,1)S(1)}, bf16[256,512]{1,0:T(8,128)(2,1)S(1)}, u32[]{:S(2)}, u32[]{:S(2)}) collective-permute-start(bf16[256,512]{1,0:T(8,128)(2,1)S(1)} %get-tuple-element.43), channel_id=1, source_target_pairs={{0,1},{1,0},{2,3},{3,2},{4,5},{5,4},{6,7},{7,6},{8,9},{9,8},{10,11... | collective-permute-start | bytes 786440 | tf_op jit(solution)/shard_map/ppermute | solution.py:330
  69.8 1.7 %collective-permute-start.24 = (bf16[256,512]{1,0:T(8,128)(2,1)S(1)}, bf16[256,512]{1,0:T(8,128)(2,1)S(1)}, u32[]{:S(2)}, u32[]{:S(2)}) collective-permute-start(bf16[256,512]{1,0:T(8,128)(2,1)S(1)} %collective-permute-done.23), channel_id=1, source_target_pairs={{0,2},{1,3},{2,4},{3,5},{4,6},{5,7},{6,0},{7,1},{8,10},{9,11},{10,... | collective-permute-start | bytes 786440 | tf_op jit(solution)/shard_map/ppermute | solution.py:330
  72.2 1.7 %collective-permute-start.15 = (bf16[256,512]{1,0:T(8,128)(2,1)S(1)}, bf16[256,512]{1,0:T(8,128)(2,1)S(1)}, u32[]{:S(2)}, u32[]{:S(2)}) collective-permute-start(bf16[256,512]{1,0:T(8,128)(2,1)S(1)} %get-tuple-element.45), channel_id=1, source_target_pairs={{0,2},{1,3},{2,4},{3,5},{4,6},{5,7},{6,0},{7,1},{8,10},{9,11},{10,... | collective-permute-start | bytes 786440 | tf_op jit(solution)/shard_map/ppermute | solution.py:330
  75.0 4.1 %collective-permute-done.20.refs_1_ = bf16[256,512]{1,0:T(8,128)(2,1)S(1)} collective-permute-done((bf16[256,512]{1,0:T(8,128)(2,1)S(1)}, bf16[256,512]{1,0:T(8,128)(2,1)S(1)}, u32[]{:S(2)}, u32[]{:S(2)}) %collective-permute-start.20) | collective-permute-done | bytes 262176 | tf_op jit(solution)/shard_map/ppermute | solution.py:330
  79.1 4.6 %collective-permute-start.8 = (bf16[256,512]{1,0:T(8,128)(2,1)S(1)}, bf16[256,512]{1,0:T(8,128)(2,1)S(1)}, u32[]{:S(2)}, u32[]{:S(2)}) collective-permute-start(bf16[256,512]{1,0:T(8,128)(2,1)S(1)} %get-tuple-element.37), channel_id=1, source_target_pairs={{0,1},{1,0},{2,3},{3,2},{4,5},{5,4},{6,7},{7,6},{8,9},{9,8},{10,11... | collective-permute-start | bytes 786440 | tf_op jit(solution)/shard_map/ppermute | solution.py:330
  87.5 4.4 %collective-permute-done.10.refs_1_ = bf16[256,512]{1,0:T(8,128)(2,1)S(1)} collective-permute-done((bf16[256,512]{1,0:T(8,128)(2,1)S(1)}, bf16[256,512]{1,0:T(8,128)(2,1)S(1)}, u32[]{:S(2)}, u32[]{:S(2)}) %collective-permute-start.10) | collective-permute-done | bytes 262176 | tf_op jit(solution)/shard_map/ppermute | solution.py:330
  92.0 1.4 %collective-permute-done.14.refs_2_ = bf16[256,512]{1,0:T(8,128)(2,1)S(1)} collective-permute-done((bf16[256,512]{1,0:T(8,128)(2,1)S(1)}, bf16[256,512]{1,0:T(8,128)(2,1)S(1)}, u32[]{:S(2)}, u32[]{:S(2)}) %collective-permute-start.14) | collective-permute-done | bytes 262176 | tf_op jit(solution)/shard_map/ppermute | solution.py:330
  (56 shorter events, 20.6 us)
Async XLA Ops:
  0.0 28.8 %collective-permute-start = (bf16[512,4096]{1,0:T(8,128)(2,1)}, bf16[512,4096]{1,0:T(8,128)(2,1)}, u32[]{:S(2)}, u32[]{:S(2)}) collective-permute-start(bf16[512,4096]{1,0:T(8,128)(2,1)} %refs_0_.6), channel_id=1, source_target_pairs={{0,1},{1,0},{2,3},{3,2},{4,5},{5,4},{6,7},{7,6},{8,9},{9,8},{10,11... | collective-permute-start | bytes 12582920 | tf_op jit(solution)/shard_map/ppermute | solution.py:345
  13.3 9.7 %collective-permute-start.1 = (bf16[512,128]{1,0:T(8,128)(2,1)S(1)}, bf16[512,128]{1,0:T(8,128)(2,1)S(1)}, u32[]{:S(2)}, u32[]{:S(2)}) collective-permute-start(bf16[512,128]{1,0:T(8,128)(2,1)S(1)} %get-tuple-element.31.refs_2_.refs_0_), channel_id=1, source_target_pairs={{0,8},{8,16},{16,24},{24,0},{32,40},{40,48},{48,56},{56,32},{64,72... | collective-permute-start | bytes 393224 | tf_op jit(solution)/shard_map/ppermute | solution.py:337
  14.7 8.3 %collective-permute-start.2 = (bf16[512,128]{1,0:T(8,128)(2,1)S(1)}, bf16[512,128]{1,0:T(8,128)(2,1)S(1)}, u32[]{:S(2)}, u32[]{:S(2)}) collective-permute-start(bf16[512,128]{1,0:T(8,128)(2,1)S(1)} %get-tuple-element.31.refs_2_.refs_0_), channel_id=1, source_target_pairs={{0,24},{8,0},{16,8},{24,16},{32,56},{40,32},{48,40},{56,48},{64,88... | collective-permute-start | bytes 393224 | tf_op jit(solution)/shard_map/ppermute | solution.py:337
  16.1 7.5 %collective-permute-start.3 = (bf16[512,128]{1,0:T(8,128)(2,1)S(1)}, bf16[512,128]{1,0:T(8,128)(2,1)S(1)}, u32[]{:S(2)}, u32[]{:S(2)}) collective-permute-start(bf16[512,128]{1,0:T(8,128)(2,1)S(1)} %get-tuple-element.31.refs_2_.refs_0_), channel_id=1, source_target_pairs={{0,16},{8,24},{16,0},{24,8},{32,48},{40,56},{48,32},{56,40},{64,80... | collective-permute-start | bytes 393224 | tf_op jit(solution)/shard_map/ppermute | solution.py:337
  23.6 8.6 %collective-permute-start.4 = (bf16[512,128]{1,0:T(8,128)(2,1)S(1)}, bf16[512,128]{1,0:T(8,128)(2,1)S(1)}, u32[]{:S(2)}, u32[]{:S(2)}) collective-permute-start(bf16[512,128]{1,0:T(8,128)(2,1)S(1)} %shard_map.66.refs_2_), channel_id=1, source_target_pairs={{0,32},{8,40},{16,48},{24,56},{32,64},{40,72},{48,80},{56,88},{64,... | collective-permute-start | bytes 393224 | tf_op jit(solution)/shard_map/ppermute | solution.py:337
  27.6 7.0 %collective-permute-start.6 = (bf16[512,128]{1,0:T(8,128)(2,1)S(1)}, bf16[512,128]{1,0:T(8,128)(2,1)S(1)}, u32[]{:S(2)}, u32[]{:S(2)}) collective-permute-start(bf16[512,128]{1,0:T(8,128)(2,1)S(1)} %shard_map.66.refs_2_), channel_id=1, source_target_pairs={{0,64},{8,72},{16,80},{24,88},{32,96},{40,104},{48,112},{56,120},{... | collective-permute-start | bytes 393224 | tf_op jit(solution)/shard_map/ppermute | solution.py:337
  35.1 9.4 %collective-permute-start.17 = (bf16[256,512]{1,0:T(8,128)(2,1)S(1)}, bf16[256,512]{1,0:T(8,128)(2,1)S(1)}, u32[]{:S(2)}, u32[]{:S(2)}) collective-permute-start(bf16[256,512]{1,0:T(8,128)(2,1)S(1)} %shard_map.78), channel_id=1, source_target_pairs={{0,1},{1,0},{2,3},{3,2},{4,5},{5,4},{6,7},{7,6},{8,9},{9,8},{10,11... | collective-permute-start | bytes 786440 | tf_op jit(solution)/shard_map/ppermute | solution.py:330
  44.9 8.5 %collective-permute-start.21 = (bf16[256,512]{1,0:T(8,128)(2,1)S(1)}, bf16[256,512]{1,0:T(8,128)(2,1)S(1)}, u32[]{:S(2)}, u32[]{:S(2)}) collective-permute-start(bf16[256,512]{1,0:T(8,128)(2,1)S(1)} %get-tuple-element.51), channel_id=1, source_target_pairs={{0,6},{1,7},{2,0},{3,1},{4,2},{5,3},{6,4},{7,5},{8,14},{9,15},{10,... | collective-permute-start | bytes 786440 | tf_op jit(solution)/shard_map/ppermute | solution.py:330
  47.7 8.3 %collective-permute-start.22 = (bf16[256,512]{1,0:T(8,128)(2,1)S(1)}, bf16[256,512]{1,0:T(8,128)(2,1)S(1)}, u32[]{:S(2)}, u32[]{:S(2)}) collective-permute-start(bf16[256,512]{1,0:T(8,128)(2,1)S(1)} %get-tuple-element.52), channel_id=1, source_target_pairs={{0,2},{1,3},{2,4},{3,5},{4,6},{5,7},{6,0},{7,1},{8,10},{9,11},{10,... | collective-permute-start | bytes 786440 | tf_op jit(solution)/shard_map/ppermute | solution.py:330
  48.4 13.2 %collective-permute-start.25 = (bf16[256,512]{1,0:T(8,128)(2,1)S(1)}, bf16[256,512]{1,0:T(8,128)(2,1)S(1)}, u32[]{:S(2)}, u32[]{:S(2)}) collective-permute-start(bf16[256,512]{1,0:T(8,128)(2,1)S(1)} %get-tuple-element.55), channel_id=1, source_target_pairs={{0,2},{1,3},{2,4},{3,5},{4,6},{5,7},{6,0},{7,1},{8,10},{9,11},{10,... | collective-permute-start | bytes 786440 | tf_op jit(solution)/shard_map/ppermute | solution.py:330
  49.9 15.3 %collective-permute-start.11 = (bf16[256,512]{1,0:T(8,128)(2,1)S(1)}, bf16[256,512]{1,0:T(8,128)(2,1)S(1)}, u32[]{:S(2)}, u32[]{:S(2)}) collective-permute-start(bf16[256,512]{1,0:T(8,128)(2,1)S(1)} %get-tuple-element.41), channel_id=1, source_target_pairs={{0,6},{1,7},{2,0},{3,1},{4,2},{5,3},{6,4},{7,5},{8,14},{9,15},{10,... | collective-permute-start | bytes 786440 | tf_op jit(solution)/shard_map/ppermute | solution.py:330
  52.6 14.6 %collective-permute-start.12 = (bf16[256,512]{1,0:T(8,128)(2,1)S(1)}, bf16[256,512]{1,0:T(8,128)(2,1)S(1)}, u32[]{:S(2)}, u32[]{:S(2)}) collective-permute-start(bf16[256,512]{1,0:T(8,128)(2,1)S(1)} %get-tuple-element.42), channel_id=1, source_target_pairs={{0,2},{1,3},{2,4},{3,5},{4,6},{5,7},{6,0},{7,1},{8,10},{9,11},{10,... | collective-permute-start | bytes 786440 | tf_op jit(solution)/shard_map/ppermute | solution.py:330
  53.4 14.6 %collective-permute-start.19 = (bf16[256,512]{1,0:T(8,128)(2,1)S(1)}, bf16[256,512]{1,0:T(8,128)(2,1)S(1)}, u32[]{:S(2)}, u32[]{:S(2)}) collective-permute-start(bf16[256,512]{1,0:T(8,128)(2,1)S(1)} %get-tuple-element.48), channel_id=1, source_target_pairs={{0,1},{1,0},{2,3},{3,2},{4,5},{5,4},{6,7},{7,6},{8,9},{9,8},{10,11... | collective-permute-start | bytes 786440 | tf_op jit(solution)/shard_map/ppermute | solution.py:330
  56.0 12.1 %collective-permute-start.18 = (bf16[256,512]{1,0:T(8,128)(2,1)S(1)}, bf16[256,512]{1,0:T(8,128)(2,1)S(1)}, u32[]{:S(2)}, u32[]{:S(2)}) collective-permute-start(bf16[256,512]{1,0:T(8,128)(2,1)S(1)} %get-tuple-element.47), channel_id=1, source_target_pairs={{0,1},{1,0},{2,3},{3,2},{4,5},{5,4},{6,7},{7,6},{8,9},{9,8},{10,11... | collective-permute-start | bytes 786440 | tf_op jit(solution)/shard_map/ppermute | solution.py:330
  61.6 8.2 %collective-permute-start.23 = (bf16[256,512]{1,0:T(8,128)(2,1)S(1)}, bf16[256,512]{1,0:T(8,128)(2,1)S(1)}, u32[]{:S(2)}, u32[]{:S(2)}) collective-permute-start(bf16[256,512]{1,0:T(8,128)(2,1)S(1)} %get-tuple-element.53), channel_id=1, source_target_pairs={{0,1},{1,0},{2,3},{3,2},{4,5},{5,4},{6,7},{7,6},{8,9},{9,8},{10,11... | collective-permute-start | bytes 786440 | tf_op jit(solution)/shard_map/ppermute | solution.py:330
  65.2 7.0 %collective-permute-start.9 = (bf16[256,512]{1,0:T(8,128)(2,1)S(1)}, bf16[256,512]{1,0:T(8,128)(2,1)S(1)}, u32[]{:S(2)}, u32[]{:S(2)}) collective-permute-start(bf16[256,512]{1,0:T(8,128)(2,1)S(1)} %get-tuple-element.38), channel_id=1, source_target_pairs={{0,1},{1,0},{2,3},{3,2},{4,5},{5,4},{6,7},{7,6},{8,9},{9,8},{10,11... | collective-permute-start | bytes 786440 | tf_op jit(solution)/shard_map/ppermute | solution.py:330
  68.0 11.1 %collective-permute-start.20 = (bf16[256,512]{1,0:T(8,128)(2,1)S(1)}, bf16[256,512]{1,0:T(8,128)(2,1)S(1)}, u32[]{:S(2)}, u32[]{:S(2)}) collective-permute-start(bf16[256,512]{1,0:T(8,128)(2,1)S(1)} %collective-permute-done.19), channel_id=1, source_target_pairs={{0,6},{1,7},{2,0},{3,1},{4,2},{5,3},{6,4},{7,5},{8,14},{9,15},{10,... | collective-permute-start | bytes 786440 | tf_op jit(solution)/shard_map/ppermute | solution.py:330
  68.0 15.6 %collective-permute-start.13 = (bf16[256,512]{1,0:T(8,128)(2,1)S(1)}, bf16[256,512]{1,0:T(8,128)(2,1)S(1)}, u32[]{:S(2)}, u32[]{:S(2)}) collective-permute-start(bf16[256,512]{1,0:T(8,128)(2,1)S(1)} %get-tuple-element.43), channel_id=1, source_target_pairs={{0,1},{1,0},{2,3},{3,2},{4,5},{5,4},{6,7},{7,6},{8,9},{9,8},{10,11... | collective-permute-start | bytes 786440 | tf_op jit(solution)/shard_map/ppermute | solution.py:330
  69.8 14.8 %collective-permute-start.24 = (bf16[256,512]{1,0:T(8,128)(2,1)S(1)}, bf16[256,512]{1,0:T(8,128)(2,1)S(1)}, u32[]{:S(2)}, u32[]{:S(2)}) collective-permute-start(bf16[256,512]{1,0:T(8,128)(2,1)S(1)} %collective-permute-done.23), channel_id=1, source_target_pairs={{0,2},{1,3},{2,4},{3,5},{4,6},{5,7},{6,0},{7,1},{8,10},{9,11},{10,... | collective-permute-start | bytes 786440 | tf_op jit(solution)/shard_map/ppermute | solution.py:330
  72.2 14.5 %collective-permute-start.15 = (bf16[256,512]{1,0:T(8,128)(2,1)S(1)}, bf16[256,512]{1,0:T(8,128)(2,1)S(1)}, u32[]{:S(2)}, u32[]{:S(2)}) collective-permute-start(bf16[256,512]{1,0:T(8,128)(2,1)S(1)} %get-tuple-element.45), channel_id=1, source_target_pairs={{0,2},{1,3},{2,4},{3,5},{4,6},{5,7},{6,0},{7,1},{8,10},{9,11},{10,... | collective-permute-start | bytes 786440 | tf_op jit(solution)/shard_map/ppermute | solution.py:330
  73.9 12.8 %collective-permute-start.16 = (bf16[256,512]{1,0:T(8,128)(2,1)S(1)}, bf16[256,512]{1,0:T(8,128)(2,1)S(1)}, u32[]{:S(2)}, u32[]{:S(2)}) collective-permute-start(bf16[256,512]{1,0:T(8,128)(2,1)S(1)} %get-tuple-element.46), channel_id=1, source_target_pairs={{0,6},{1,7},{2,0},{3,1},{4,2},{5,3},{6,4},{7,5},{8,14},{9,15},{10,... | collective-permute-start | bytes 786440 | tf_op jit(solution)/shard_map/ppermute | solution.py:330
  79.1 8.5 %collective-permute-start.8 = (bf16[256,512]{1,0:T(8,128)(2,1)S(1)}, bf16[256,512]{1,0:T(8,128)(2,1)S(1)}, u32[]{:S(2)}, u32[]{:S(2)}) collective-permute-start(bf16[256,512]{1,0:T(8,128)(2,1)S(1)} %get-tuple-element.37), channel_id=1, source_target_pairs={{0,1},{1,0},{2,3},{3,2},{4,5},{5,4},{6,7},{7,6},{8,9},{9,8},{10,11... | collective-permute-start | bytes 786440 | tf_op jit(solution)/shard_map/ppermute | solution.py:330
  83.6 8.3 %collective-permute-start.10 = (bf16[256,512]{1,0:T(8,128)(2,1)S(1)}, bf16[256,512]{1,0:T(8,128)(2,1)S(1)}, u32[]{:S(2)}, u32[]{:S(2)}) collective-permute-start(bf16[256,512]{1,0:T(8,128)(2,1)S(1)} %collective-permute-done.9), channel_id=1, source_target_pairs={{0,6},{1,7},{2,0},{3,1},{4,2},{5,3},{6,4},{7,5},{8,14},{9,15},{10,... | collective-permute-start | bytes 786440 | tf_op jit(solution)/shard_map/ppermute | solution.py:330
  84.6 8.8 %collective-permute-start.14 = (bf16[256,512]{1,0:T(8,128)(2,1)S(1)}, bf16[256,512]{1,0:T(8,128)(2,1)S(1)}, u32[]{:S(2)}, u32[]{:S(2)}) collective-permute-start(bf16[256,512]{1,0:T(8,128)(2,1)S(1)} %collective-permute-done.13), channel_id=1, source_target_pairs={{0,2},{1,3},{2,4},{3,5},{4,6},{5,7},{6,0},{7,1},{8,10},{9,11},{10,... | collective-permute-start | bytes 786440 | tf_op jit(solution)/shard_map/ppermute | solution.py:330
  (4 other events, 25.5 us)
where the time goes:
time: 94.4 us; the launch traced here: 94.2 us
  Pallas kernels  38.2 us (40%)
  starting transfers between devices  37.8 us (40%)
  waiting for transfers between devices  17.9 us (19%)
    pallas_call x20, Pallas kernels, call(): pl.pallas_call(kernel, in_specs=in_specs, out_specs=jax.tree.map(lambda _...  35 us
    ppermute x20, starting transfers between devices, head_send(): return held(lax.ppermute(x, 'head', pairs))  26.9 us
    ppermute x20, waiting for transfers between devices, head_send(): return held(lax.ppermute(x, 'head', pairs))  15.1 us
    ppermute x6, starting transfers between devices, seq_send(): return held(lax.ppermute(x, 'seq', pairs))  9.52 us
    pallas_call x4, Pallas kernels, final_sum(): pl.pallas_call(kernel, grid_spec=pltpu.PrefetchScalarGridSpec(num_scalar_...  3.2 us
    ppermute x6, waiting for transfers between devices, seq_send(): return held(lax.ppermute(x, 'seq', pairs))  2.8 us
  transfers between devices with their start and end apart: 27, of which 8 were waited for; matrix products, arithmetic and copies ran while one was open for 0% of the time, Pallas kernels for 39%

commit v1 on v0

--- a/solution.py
+++ b/solution.py
@@ -9,7 +9,7 @@
 HEAD_DIM = 128
 BLOCK = 256
 RING = 4
-SETS = 2
+SETS = 1
 F32, BF16 = jnp.float32, jnp.bfloat16
 IN_VMEM = pl.BlockSpec(memory_space=pltpu.VMEM)
 IN_HBM = pl.BlockSpec(memory_space=pltpu.HBM)
@@ -256,6 +256,15 @@
 
 
 STRAIGHT, CROSS = 0, 1
+OWN, OUTER, INNER, FAR = range(4)
+
+
+def chip_of(step, y):
+    if step == OUTER:
+        return RING - 1 - y
+    if step == INNER:
+        return y + 1 - 2 * (y % 2)
+    return y if step == OWN else (y + 2) % RING
 
 
 def out_project(place, mine, theirs, w_out, blocks, added=(), partial=False):
@@ -267,7 +276,7 @@
         adds, outs = refs[: len(added)], refs[len(added) :]
         y, c = place_ref[0] // 2, place_ref[0] % 2
         for p, (step, side) in enumerate(blocks):
-            owner = ((y + step + RING) % RING) * 2 + (c if side == STRAIGHT else 1 - c)
+            owner = chip_of(step, y) * 2 + (c if side == STRAIGHT else 1 - c)
             cols = pl.ds(pl.multiple_of(owner * width, width), width)
             total = adds[p][...].astype(F32) if added else 0.0
             if mine is not None:
@@ -325,7 +334,7 @@
 
 def head_send(x, step, cross=0):
     pairs = [
-        (h, ((h // 2 + step) % RING) * 2 + ((h % 2) ^ cross)) for h in range(2 * RING)
+        (h, chip_of(step, h // 2) * 2 + ((h % 2) ^ cross)) for h in range(2 * RING)
     ]
     return held(lax.ppermute(x, "head", pairs))
 
@@ -371,7 +380,7 @@
             return head_send(x, step)
 
         def swap(x):
-            return head_send(x, 0, 1)
+            return head_send(x, OWN, 1)
 
         theirs = swap(attended(False))
         mine = attended(True)
@@ -379,18 +388,20 @@
         def project_out(blocks, mine=mine, theirs=theirs, **kw):
             return out_project(place, mine, theirs, w_held, blocks, **kw)
 
-        blocks = [(2, STRAIGHT), (2, CROSS)]
+        blocks = [(FAR, STRAIGHT), (FAR, CROSS)]
         begun = project_out(blocks, theirs=None, partial=True)
         far_s, far_x = project_out(blocks, mine=None, added=begun)
-        far_s, far_x = send(far_s, -1), send(far_x, 1)
-        near_s, near_x = project_out([(1, STRAIGHT), (-1, CROSS)])
-        near_s, near_x = send(near_s, 1), send(swap(near_x), -1)
-        own_s, own_x = project_out([(0, STRAIGHT), (0, CROSS)])
+        far_s, far_x = send(far_s, OUTER), send(far_x, INNER)
+        near_s, near_x = project_out([(OUTER, STRAIGHT), (INNER, CROSS)])
+        near_s = send(near_s, OUTER)
+        near_x = send(swap(near_x), INNER)
+        own_s, own_x = project_out([(OWN, STRAIGHT), (OWN, CROSS)])
         own_x = swap(own_x)
-        late_s, late_x = project_out([(-1, STRAIGHT), (1, CROSS)], added=(far_s, far_x))
-        late_s, late_x = send(late_s, -1), send(swap(late_x), 1)
+        late_s, late_x = project_out([(INNER, STRAIGHT), (OUTER, CROSS)], added=(far_s, far_x))
+        late_s = send(late_s, INNER)
+        late_x = send(swap(late_x), OUTER)
+        out = final_sum(place, part, True, (own_x, near_x, late_x), count, into=out)
         out = final_sum(place, part, False, (own_s, near_s, late_s), count, into=out)
-        out = final_sum(place, part, True, (own_x, near_x, late_x), count, into=out)
     return out
 
 

time: 94.4 us -> 86.6 us (0.917)
  starting transfers between devices: 37.8 us -> 21.2 us
  waiting for transfers between devices: 17.9 us -> 34.1 us
  Pallas kernels: 38.2 us -> 30.9 us
    ppermute x20 -> x10, waiting for transfers between devices: 15.1 us -> 31.9 us  [head_send(): return held(lax.ppermute(x, 'head', pairs))]
    ppermute x20 -> x10, starting transfers between devices: 26.9 us -> 10.3 us  [head_send(): return held(lax.ppermute(x, 'head', pairs))]
    pallas_call x20 -> x11, Pallas kernels: 35 us -> 29 us  [call(): pl.pallas_call(kernel, in_specs=in_specs, out_specs=jax.tree.map(lambda _...]
    pallas_call x4 -> x2, Pallas kernels: 3.2 us -> 1.96 us  [final_sum(): pl.pallas_call(kernel, grid_spec=pltpu.PrefetchScalarGridSpec(num_scalar_...]
  transfers between devices with their start and end apart: 27 -> 17, of which waited for: 8 -> 8; matrix products, arithmetic and copies ran while one was open for 0% -> 0% of each run, Pallas kernels for 39% -> 33%
where the time goes in v1:
time: 86.6 us; the launch traced here: 86.5 us
  waiting for transfers between devices  34.1 us (39%)
  Pallas kernels  30.9 us (36%)
  starting transfers between devices  21.2 us (24%)
    ppermute x10, waiting for transfers between devices, head_send(): return held(lax.ppermute(x, 'head', pairs))  31.9 us
    pallas_call x11, Pallas kernels, call(): pl.pallas_call(kernel, in_specs=in_specs, out_specs=jax.tree.map(lambda _...  29 us
    ppermute x10, starting transfers between devices, head_send(): return held(lax.ppermute(x, 'head', pairs))  10.3 us
    ppermute x6, starting transfers between devices, seq_send(): return held(lax.ppermute(x, 'seq', pairs))  9.53 us
    ppermute x6, waiting for transfers between devices, seq_send(): return held(lax.ppermute(x, 'seq', pairs))  2.27 us
    pallas_call x2, Pallas kernels, final_sum(): pl.pallas_call(kernel, grid_spec=pltpu.PrefetchScalarGridSpec(num_scalar_...  1.96 us
  transfers between devices with their start and end apart: 17, of which 8 were waited for; matrix products, arithmetic and copies ran while one was open for 0% of the time, Pallas kernels for 33%

profile of v1, /device:TPU:1, one launch (start us, length us, event | category | flops | bytes accessed | tf_op | source)
XLA Modules:
  0.0 86.5 jit_solution(162721670461052088)
XLA Ops:
  0.0 1.4 %collective-permute-start = (bf16[512,4096]{1,0:T(8,128)(2,1)}, bf16[512,4096]{1,0:T(8,128)(2,1)}, u32[]{:S(2)}, u32[]{:S(2)}) collective-permute-start(bf16[512,4096]{1,0:T(8,128)(2,1)} %refs_0_.5), channel_id=1, source_target_pairs={{0,1},{1,0},{2,3},{3,2},{4,5},{5,4},{6,7},{7,6},{8,9},{9,8},{10,11... | collective-permute-start | bytes 12582920 | tf_op jit(solution)/shard_map/ppermute | solution.py:354
  1.4 12.0 %shard_map.64 = (bf16[1024,512]{1,0:T(8,128)(2,1)S(1)}, bf16[1024,512]{1,0:T(8,128)(2,1)S(1)}, bf16[512,128]{1,0:T(8,128)(2,1)S(1)}) custom-call(bf16[1024,4096]{1,0:T(8,128)(2,1)} %refs_0_.4, bf16[4096,512]{1,0:T(8,128)(2,1)} %refs_1_.2, bf16[4096,512]{1,0:T(8,128)(2,1)} %refs_2_.1, s32[1]{0:T(128)} %bitcast.refs_3_.place_ref, s32[1]{0:T(128)} %bitcast.1.refs_4_.index_ref), custom_call_target="tpu_custom_call" | custom-call | flops 8589934592 | bytes 16777216 | tf_op jit(solution)/shard_map/pallas_call | solution.py:28
  13.4 1.4 %collective-permute-start.1 = (bf16[512,128]{1,0:T(8,128)(2,1)S(1)}, bf16[512,128]{1,0:T(8,128)(2,1)S(1)}, u32[]{:S(2)}, u32[]{:S(2)}) collective-permute-start(bf16[512,128]{1,0:T(8,128)(2,1)S(1)} %get-tuple-element.21.refs_2_.refs_0_), channel_id=1, source_target_pairs={{0,8},{8,16},{16,24},{24,0},{32,40},{40,48},{48,56},{56,32},{64,72... | collective-permute-start | bytes 393224 | tf_op jit(solution)/shard_map/ppermute | solution.py:346
  14.8 1.3 %collective-permute-start.2 = (bf16[512,128]{1,0:T(8,128)(2,1)S(1)}, bf16[512,128]{1,0:T(8,128)(2,1)S(1)}, u32[]{:S(2)}, u32[]{:S(2)}) collective-permute-start(bf16[512,128]{1,0:T(8,128)(2,1)S(1)} %get-tuple-element.21.refs_2_.refs_0_), channel_id=1, source_target_pairs={{0,24},{8,0},{16,8},{24,16},{32,56},{40,32},{48,40},{56,48},{64,88... | collective-permute-start | bytes 393224 | tf_op jit(solution)/shard_map/ppermute | solution.py:346
  16.2 1.6 %collective-permute-start.3 = (bf16[512,128]{1,0:T(8,128)(2,1)S(1)}, bf16[512,128]{1,0:T(8,128)(2,1)S(1)}, u32[]{:S(2)}, u32[]{:S(2)}) collective-permute-start(bf16[512,128]{1,0:T(8,128)(2,1)S(1)} %get-tuple-element.21.refs_2_.refs_0_), channel_id=1, source_target_pairs={{0,16},{8,24},{16,0},{24,8},{32,48},{40,56},{48,32},{56,40},{64,80... | collective-permute-start | bytes 393224 | tf_op jit(solution)/shard_map/ppermute | solution.py:346
  17.8 7.0 %shard_map.65.refs_4_.q_ref = bf16[1024,512]{1,0:T(8,128)(2,1)S(1)} custom-call(bf16[1024,4096]{1,0:T(8,128)(2,1)} %refs_0_.4, bf16[4096,512]{1,0:T(8,128)(2,1)} %refs_1_.3, bf16[512,128]{1,0:T(8,128)(2,1)S(1)} %get-tuple-element.21.refs_2_.refs_0_), custom_call_target="tpu_custom_call" | custom-call | flops 4294967296 | bytes 12582912 | tf_op jit(solution)/shard_map/pallas_call | solution.py:28
  24.9 1.7 %collective-permute-start.4 = (bf16[512,128]{1,0:T(8,128)(2,1)S(1)}, bf16[512,128]{1,0:T(8,128)(2,1)S(1)}, u32[]{:S(2)}, u32[]{:S(2)}) collective-permute-start(bf16[512,128]{1,0:T(8,128)(2,1)S(1)} %shard_map.66.refs_2_), channel_id=1, source_target_pairs={{0,32},{8,40},{16,48},{24,56},{32,64},{40,72},{48,80},{56,88},{64,... | collective-permute-start | bytes 393224 | tf_op jit(solution)/shard_map/ppermute | solution.py:346
  26.6 2.2 %collective-permute-start.5 = (bf16[512,128]{1,0:T(8,128)(2,1)S(1)}, bf16[512,128]{1,0:T(8,128)(2,1)S(1)}, u32[]{:S(2)}, u32[]{:S(2)}) collective-permute-start(bf16[512,128]{1,0:T(8,128)(2,1)S(1)} %shard_map.66.refs_2_), channel_id=1, source_target_pairs={{0,96},{8,104},{16,112},{24,120},{32,0},{40,8},{48,16},{56,24},{64... | collective-permute-start | bytes 393224 | tf_op jit(solution)/shard_map/ppermute | solution.py:346
  28.8 1.2 %collective-permute-start.6 = (bf16[512,128]{1,0:T(8,128)(2,1)S(1)}, bf16[512,128]{1,0:T(8,128)(2,1)S(1)}, u32[]{:S(2)}, u32[]{:S(2)}) collective-permute-start(bf16[512,128]{1,0:T(8,128)(2,1)S(1)} %shard_map.66.refs_2_), channel_id=1, source_target_pairs={{0,64},{8,72},{16,80},{24,88},{32,96},{40,104},{48,112},{56,120},{... | collective-permute-start | bytes 393224 | tf_op jit(solution)/shard_map/ppermute | solution.py:346
  30.0 3.5 %shard_map.67 = (f32[1024,512]{1,0:T(8,128)S(1)}, f32[4,512,128]{2,1,0:T(8,128)S(1)}, bf16[1024,4096]{1,0:T(8,128)(2,1)S(1)}) custom-call(bf16[1024,512]{1,0:T(8,128)(2,1)S(1)} %shard_map.65.refs_4_.q_ref, bf16[1024,512]{1,0:T(8,128)(2,1)S(1)} %get-tuple-element.22.k_ref, bf16[1024,512]{1,0:T(8,128)(2,1)S(1)} %get-tuple-element.23.v_ref, ...), custom_call_target="tpu_custom_call" | custom-call | flops 805306368 | bytes 15728640 | tf_op jit(solution)/shard_map/pallas_call | solution.py:28
  33.6 2.3 %collective-permute-done.6.refs_5_ = bf16[512,128]{1,0:T(8,128)(2,1)S(1)} collective-permute-done((bf16[512,128]{1,0:T(8,128)(2,1)S(1)}, bf16[512,128]{1,0:T(8,128)(2,1)S(1)}, u32[]{:S(2)}, u32[]{:S(2)}) %collective-permute-start.6) | collective-permute-done | bytes 131104 | tf_op jit(solution)/shard_map/ppermute | solution.py:346
  36.4 1.4 %collective-permute-start.7 = (bf16[512,512]{1,0:T(8,128)(2,1)S(1)}, bf16[512,512]{1,0:T(8,128)(2,1)S(1)}, u32[]{:S(2)}, u32[]{:S(2)}) collective-permute-start(bf16[512,512]{1,0:T(8,128)(2,1)S(1)} %shard_map.69), channel_id=1, source_target_pairs={{0,1},{1,0},{2,3},{3,2},{4,5},{5,4},{6,7},{7,6},{8,9},{9,8},{10,11... | collective-permute-start | bytes 1572872 | tf_op jit(solution)/shard_map/ppermute | solution.py:339
  40.1 1.4 %collective-permute-start.10 = (bf16[512,512]{1,0:T(8,128)(2,1)S(1)}, bf16[512,512]{1,0:T(8,128)(2,1)S(1)}, u32[]{:S(2)}, u32[]{:S(2)}) collective-permute-start(bf16[512,512]{1,0:T(8,128)(2,1)S(1)} %get-tuple-element.32), channel_id=1, source_target_pairs={{0,2},{1,3},{2,0},{3,1},{4,6},{5,7},{6,4},{7,5},{8,10},{9,11},{10,... | collective-permute-start | bytes 1572872 | tf_op jit(solution)/shard_map/ppermute | solution.py:339
  41.5 1.9 %collective-permute-start.9 = (bf16[512,512]{1,0:T(8,128)(2,1)S(1)}, bf16[512,512]{1,0:T(8,128)(2,1)S(1)}, u32[]{:S(2)}, u32[]{:S(2)}) collective-permute-start(bf16[512,512]{1,0:T(8,128)(2,1)S(1)} %get-tuple-element.31), channel_id=1, source_target_pairs={{0,6},{1,7},{2,4},{3,5},{4,2},{5,3},{6,0},{7,1},{8,14},{9,15},{10,... | collective-permute-start | bytes 1572872 | tf_op jit(solution)/shard_map/ppermute | solution.py:339
  43.4 1.2 %shard_map.71 = (bf16[512,512]{1,0:T(8,128)(2,1)S(1)}, bf16[512,512]{1,0:T(8,128)(2,1)S(1)}) custom-call(s32[1]{0:T(128)} %bitcast.refs_3_.place_ref, bf16[512,512]{1,0:T(8,128)(2,1)S(1)} %shard_map.68.refs_0_, bf16[512,512]{1,0:T(8,128)(2,1)S(1)} %collective-permute-done.7.refs_1_.refs_0_, bf16[1024,4096]{1,0:T(8,128)(2,1)S(1)} %get-tuple-element.26.refs_2_.refs_1_), custom_call_target="tpu_custom_call" | custom-call | flops 1073741824 | bytes 2097152 | tf_op jit(solution)/shard_map/pallas_call | solution.py:28
  45.7 7.6 %collective-permute-done.10.refs_4_ = bf16[512,512]{1,0:T(8,128)(2,1)S(1)} collective-permute-done((bf16[512,512]{1,0:T(8,128)(2,1)S(1)}, bf16[512,512]{1,0:T(8,128)(2,1)S(1)}, u32[]{:S(2)}, u32[]{:S(2)}) %collective-permute-start.10) | collective-permute-done | bytes 524320 | tf_op jit(solution)/shard_map/ppermute | solution.py:339
  53.3 2.2 %collective-permute-done.9.refs_3_ = bf16[512,512]{1,0:T(8,128)(2,1)S(1)} collective-permute-done((bf16[512,512]{1,0:T(8,128)(2,1)S(1)}, bf16[512,512]{1,0:T(8,128)(2,1)S(1)}, u32[]{:S(2)}, u32[]{:S(2)}) %collective-permute-start.9) | collective-permute-done | bytes 524320 | tf_op jit(solution)/shard_map/ppermute | solution.py:339
  55.5 1.3 %shard_map.74 = (bf16[512,512]{1,0:T(8,128)(2,1)S(1)}, bf16[512,512]{1,0:T(8,128)(2,1)S(1)}) custom-call(s32[1]{0:T(128)} %bitcast.refs_3_.place_ref, bf16[512,512]{1,0:T(8,128)(2,1)S(1)} %shard_map.68.refs_0_, bf16[512,512]{1,0:T(8,128)(2,1)S(1)} %collective-permute-done.7.refs_1_.refs_0_, bf16[1024,4096]{1,0:T(8,128)(2,1)S(1)} %get-tuple-element.26.refs_2_.refs_1_, ...), custom_call_target="tpu_custom_call" | custom-call | flops 1073741824 | bytes 2097152 | tf_op jit(solution)/shard_map/pallas_call | solution.py:28
  56.8 1.6 %collective-permute-start.15 = (bf16[512,512]{1,0:T(8,128)(2,1)S(1)}, bf16[512,512]{1,0:T(8,128)(2,1)S(1)}, u32[]{:S(2)}, u32[]{:S(2)}) collective-permute-start(bf16[512,512]{1,0:T(8,128)(2,1)S(1)} %get-tuple-element.36), channel_id=1, source_target_pairs={{0,1},{1,0},{2,3},{3,2},{4,5},{5,4},{6,7},{7,6},{8,9},{9,8},{10,11... | collective-permute-start | bytes 1572872 | tf_op jit(solution)/shard_map/ppermute | solution.py:339
  58.4 1.2 %shard_map.70 = (bf16[512,512]{1,0:T(8,128)(2,1)S(1)}, bf16[512,512]{1,0:T(8,128)(2,1)S(1)}) custom-call(s32[1]{0:T(128)} %bitcast.refs_3_.place_ref, bf16[512,512]{1,0:T(8,128)(2,1)S(1)} %shard_map.68.refs_0_, bf16[512,512]{1,0:T(8,128)(2,1)S(1)} %collective-permute-done.7.refs_1_.refs_0_, bf16[1024,4096]{1,0:T(8,128)(2,1)S(1)} %get-tuple-element.26.refs_2_.refs_1_), custom_call_target="tpu_custom_call" | custom-call | flops 1073741824 | bytes 2097152 | tf_op jit(solution)/shard_map/pallas_call | solution.py:28
  59.9 1.9 %collective-permute-start.16 = (bf16[512,512]{1,0:T(8,128)(2,1)S(1)}, bf16[512,512]{1,0:T(8,128)(2,1)S(1)}, u32[]{:S(2)}, u32[]{:S(2)}) collective-permute-start(bf16[512,512]{1,0:T(8,128)(2,1)S(1)} %collective-permute-done.15), channel_id=1, source_target_pairs={{0,6},{1,7},{2,4},{3,5},{4,2},{5,3},{6,0},{7,1},{8,14},{9,15},{10,... | collective-permute-start | bytes 1572872 | tf_op jit(solution)/shard_map/ppermute | solution.py:339
  62.8 10.1 %collective-permute-done.14.refs_1_ = bf16[512,512]{1,0:T(8,128)(2,1)S(1)} collective-permute-done((bf16[512,512]{1,0:T(8,128)(2,1)S(1)}, bf16[512,512]{1,0:T(8,128)(2,1)S(1)}, u32[]{:S(2)}, u32[]{:S(2)}) %collective-permute-start.14) | collective-permute-done | bytes 524320 | tf_op jit(solution)/shard_map/ppermute | solution.py:339
  72.9 1.3 %collective-permute-done.16.refs_2_ = bf16[512,512]{1,0:T(8,128)(2,1)S(1)} collective-permute-done((bf16[512,512]{1,0:T(8,128)(2,1)S(1)}, bf16[512,512]{1,0:T(8,128)(2,1)S(1)}, u32[]{:S(2)}, u32[]{:S(2)}) %collective-permute-start.16) | collective-permute-done | bytes 524320 | tf_op jit(solution)/shard_map/ppermute | solution.py:339
  75.2 10.3 %collective-permute-done.8.refs_1_ = bf16[512,512]{1,0:T(8,128)(2,1)S(1)} collective-permute-done((bf16[512,512]{1,0:T(8,128)(2,1)S(1)}, bf16[512,512]{1,0:T(8,128)(2,1)S(1)}, u32[]{:S(2)}, u32[]{:S(2)}) %collective-permute-start.8) | collective-permute-done | bytes 524320 | tf_op jit(solution)/shard_map/ppermute | solution.py:339
  (25 shorter events, 7.1 us)
Async XLA Ops:
  0.0 30.0 %collective-permute-start = (bf16[512,4096]{1,0:T(8,128)(2,1)}, bf16[512,4096]{1,0:T(8,128)(2,1)}, u32[]{:S(2)}, u32[]{:S(2)}) collective-permute-start(bf16[512,4096]{1,0:T(8,128)(2,1)} %refs_0_.5), channel_id=1, source_target_pairs={{0,1},{1,0},{2,3},{3,2},{4,5},{5,4},{6,7},{7,6},{8,9},{9,8},{10,11... | collective-permute-start | bytes 12582920 | tf_op jit(solution)/shard_map/ppermute | solution.py:354
  13.4 11.4 %collective-permute-start.1 = (bf16[512,128]{1,0:T(8,128)(2,1)S(1)}, bf16[512,128]{1,0:T(8,128)(2,1)S(1)}, u32[]{:S(2)}, u32[]{:S(2)}) collective-permute-start(bf16[512,128]{1,0:T(8,128)(2,1)S(1)} %get-tuple-element.21.refs_2_.refs_0_), channel_id=1, source_target_pairs={{0,8},{8,16},{16,24},{24,0},{32,40},{40,48},{48,56},{56,32},{64,72... | collective-permute-start | bytes 393224 | tf_op jit(solution)/shard_map/ppermute | solution.py:346
  14.8 10.0 %collective-permute-start.2 = (bf16[512,128]{1,0:T(8,128)(2,1)S(1)}, bf16[512,128]{1,0:T(8,128)(2,1)S(1)}, u32[]{:S(2)}, u32[]{:S(2)}) collective-permute-start(bf16[512,128]{1,0:T(8,128)(2,1)S(1)} %get-tuple-element.21.refs_2_.refs_0_), channel_id=1, source_target_pairs={{0,24},{8,0},{16,8},{24,16},{32,56},{40,32},{48,40},{56,48},{64,88... | collective-permute-start | bytes 393224 | tf_op jit(solution)/shard_map/ppermute | solution.py:346
  16.2 8.7 %collective-permute-start.3 = (bf16[512,128]{1,0:T(8,128)(2,1)S(1)}, bf16[512,128]{1,0:T(8,128)(2,1)S(1)}, u32[]{:S(2)}, u32[]{:S(2)}) collective-permute-start(bf16[512,128]{1,0:T(8,128)(2,1)S(1)} %get-tuple-element.21.refs_2_.refs_0_), channel_id=1, source_target_pairs={{0,16},{8,24},{16,0},{24,8},{32,48},{40,56},{48,32},{56,40},{64,80... | collective-permute-start | bytes 393224 | tf_op jit(solution)/shard_map/ppermute | solution.py:346
  24.9 8.6 %collective-permute-start.4 = (bf16[512,128]{1,0:T(8,128)(2,1)S(1)}, bf16[512,128]{1,0:T(8,128)(2,1)S(1)}, u32[]{:S(2)}, u32[]{:S(2)}) collective-permute-start(bf16[512,128]{1,0:T(8,128)(2,1)S(1)} %shard_map.66.refs_2_), channel_id=1, source_target_pairs={{0,32},{8,40},{16,48},{24,56},{32,64},{40,72},{48,80},{56,88},{64,... | collective-permute-start | bytes 393224 | tf_op jit(solution)/shard_map/ppermute | solution.py:346
  26.6 7.0 %collective-permute-start.5 = (bf16[512,128]{1,0:T(8,128)(2,1)S(1)}, bf16[512,128]{1,0:T(8,128)(2,1)S(1)}, u32[]{:S(2)}, u32[]{:S(2)}) collective-permute-start(bf16[512,128]{1,0:T(8,128)(2,1)S(1)} %shard_map.66.refs_2_), channel_id=1, source_target_pairs={{0,96},{8,104},{16,112},{24,120},{32,0},{40,8},{48,16},{56,24},{64... | collective-permute-start | bytes 393224 | tf_op jit(solution)/shard_map/ppermute | solution.py:346
  28.8 7.0 %collective-permute-start.6 = (bf16[512,128]{1,0:T(8,128)(2,1)S(1)}, bf16[512,128]{1,0:T(8,128)(2,1)S(1)}, u32[]{:S(2)}, u32[]{:S(2)}) collective-permute-start(bf16[512,128]{1,0:T(8,128)(2,1)S(1)} %shard_map.66.refs_2_), channel_id=1, source_target_pairs={{0,64},{8,72},{16,80},{24,88},{32,96},{40,104},{48,112},{56,120},{... | collective-permute-start | bytes 393224 | tf_op jit(solution)/shard_map/ppermute | solution.py:346
  30.0 5.8 %copy-start = (f32[512]{0:T(512)S(1)}, f32[512]{0:T(512)}, u32[]{:S(2)}) copy-start(f32[512]{0:T(512)} %param.10) | copy-start | bytes 6148
  36.4 3.0 %collective-permute-start.7 = (bf16[512,512]{1,0:T(8,128)(2,1)S(1)}, bf16[512,512]{1,0:T(8,128)(2,1)S(1)}, u32[]{:S(2)}, u32[]{:S(2)}) collective-permute-start(bf16[512,512]{1,0:T(8,128)(2,1)S(1)} %shard_map.69), channel_id=1, source_target_pairs={{0,1},{1,0},{2,3},{3,2},{4,5},{5,4},{6,7},{7,6},{8,9},{9,8},{10,11... | collective-permute-start | bytes 1572872 | tf_op jit(solution)/shard_map/ppermute | solution.py:339
  40.1 13.2 %collective-permute-start.10 = (bf16[512,512]{1,0:T(8,128)(2,1)S(1)}, bf16[512,512]{1,0:T(8,128)(2,1)S(1)}, u32[]{:S(2)}, u32[]{:S(2)}) collective-permute-start(bf16[512,512]{1,0:T(8,128)(2,1)S(1)} %get-tuple-element.32), channel_id=1, source_target_pairs={{0,2},{1,3},{2,0},{3,1},{4,6},{5,7},{6,4},{7,5},{8,10},{9,11},{10,... | collective-permute-start | bytes 1572872 | tf_op jit(solution)/shard_map/ppermute | solution.py:339
  41.5 14.0 %collective-permute-start.9 = (bf16[512,512]{1,0:T(8,128)(2,1)S(1)}, bf16[512,512]{1,0:T(8,128)(2,1)S(1)}, u32[]{:S(2)}, u32[]{:S(2)}) collective-permute-start(bf16[512,512]{1,0:T(8,128)(2,1)S(1)} %get-tuple-element.31), channel_id=1, source_target_pairs={{0,6},{1,7},{2,4},{3,5},{4,2},{5,3},{6,0},{7,1},{8,14},{9,15},{10,... | collective-permute-start | bytes 1572872 | tf_op jit(solution)/shard_map/ppermute | solution.py:339
  44.7 15.1 %collective-permute-start.13 = (bf16[512,512]{1,0:T(8,128)(2,1)S(1)}, bf16[512,512]{1,0:T(8,128)(2,1)S(1)}, u32[]{:S(2)}, u32[]{:S(2)}) collective-permute-start(bf16[512,512]{1,0:T(8,128)(2,1)S(1)} %get-tuple-element.35), channel_id=1, source_target_pairs={{0,1},{1,0},{2,3},{3,2},{4,5},{5,4},{6,7},{7,6},{8,9},{9,8},{10,11... | collective-permute-start | bytes 1572872 | tf_op jit(solution)/shard_map/ppermute | solution.py:339
  56.8 3.1 %collective-permute-start.15 = (bf16[512,512]{1,0:T(8,128)(2,1)S(1)}, bf16[512,512]{1,0:T(8,128)(2,1)S(1)}, u32[]{:S(2)}, u32[]{:S(2)}) collective-permute-start(bf16[512,512]{1,0:T(8,128)(2,1)S(1)} %get-tuple-element.36), channel_id=1, source_target_pairs={{0,1},{1,0},{2,3},{3,2},{4,5},{5,4},{6,7},{7,6},{8,9},{9,8},{10,11... | collective-permute-start | bytes 1572872 | tf_op jit(solution)/shard_map/ppermute | solution.py:339
  59.6 3.1 %collective-permute-start.12 = (bf16[512,512]{1,0:T(8,128)(2,1)S(1)}, bf16[512,512]{1,0:T(8,128)(2,1)S(1)}, u32[]{:S(2)}, u32[]{:S(2)}) collective-permute-start(bf16[512,512]{1,0:T(8,128)(2,1)S(1)} %get-tuple-element.34), channel_id=1, source_target_pairs={{0,1},{1,0},{2,3},{3,2},{4,5},{5,4},{6,7},{7,6},{8,9},{9,8},{10,11... | collective-permute-start | bytes 1572872 | tf_op jit(solution)/shard_map/ppermute | solution.py:339
  59.8 13.1 %collective-permute-start.14 = (bf16[512,512]{1,0:T(8,128)(2,1)S(1)}, bf16[512,512]{1,0:T(8,128)(2,1)S(1)}, u32[]{:S(2)}, u32[]{:S(2)}) collective-permute-start(bf16[512,512]{1,0:T(8,128)(2,1)S(1)} %collective-permute-done.13), channel_id=1, source_target_pairs={{0,2},{1,3},{2,0},{3,1},{4,6},{5,7},{6,4},{7,5},{8,10},{9,11},{10,... | collective-permute-start | bytes 1572872 | tf_op jit(solution)/shard_map/ppermute | solution.py:339
  59.9 14.3 %collective-permute-start.16 = (bf16[512,512]{1,0:T(8,128)(2,1)S(1)}, bf16[512,512]{1,0:T(8,128)(2,1)S(1)}, u32[]{:S(2)}, u32[]{:S(2)}) collective-permute-start(bf16[512,512]{1,0:T(8,128)(2,1)S(1)} %collective-permute-done.15), channel_id=1, source_target_pairs={{0,6},{1,7},{2,4},{3,5},{4,2},{5,3},{6,0},{7,1},{8,14},{9,15},{10,... | collective-permute-start | bytes 1572872 | tf_op jit(solution)/shard_map/ppermute | solution.py:339
  61.8 23.6 %collective-permute-start.8 = (bf16[512,512]{1,0:T(8,128)(2,1)S(1)}, bf16[512,512]{1,0:T(8,128)(2,1)S(1)}, u32[]{:S(2)}, u32[]{:S(2)}) collective-permute-start(bf16[512,512]{1,0:T(8,128)(2,1)S(1)} %get-tuple-element.28), channel_id=1, source_target_pairs={{0,6},{1,7},{2,4},{3,5},{4,2},{5,3},{6,0},{7,1},{8,14},{9,15},{10,... | collective-permute-start | bytes 1572872 | tf_op jit(solution)/shard_map/ppermute | solution.py:339
  62.6 22.9 %collective-permute-start.11 = (bf16[512,512]{1,0:T(8,128)(2,1)S(1)}, bf16[512,512]{1,0:T(8,128)(2,1)S(1)}, u32[]{:S(2)}, u32[]{:S(2)}) collective-permute-start(bf16[512,512]{1,0:T(8,128)(2,1)S(1)} %get-tuple-element.33), channel_id=1, source_target_pairs={{0,2},{1,3},{2,0},{3,1},{4,6},{5,7},{6,4},{7,5},{8,10},{9,11},{10,... | collective-permute-start | bytes 1572872 | tf_op jit(solution)/shard_map/ppermute | solution.py:339
